TPU v7x, 32 devices: a whole 2x2x4 slice. The times are simulated.
32 devices in a mesh: dp: 8 (over y, x, core), seq: 4 (over z).
Axes of the slice: x: 2, y: 2, z: 4, core: 2. Of those that a mesh axis runs over, the one named last changes fastest.
Arguments:
- tokens: bfloat16 [8, 512, 1024], P('dp', 'seq'), may hold values from -6 to 6
- prefix_len: int32 [8], P('dp'), may hold values from 51 to 256
- routes: int32 [8, 512, 8], P('dp', 'seq'), may hold values from 0 to 15, all different within a row; in each aligned block of 128 rows (0 to 127, 128 to 255, ..., all dimensions but the last counted through in order) at most 96 rows name the same one
- cotangent: bfloat16 [8, 512, 1024], P('dp', 'seq'), may hold values from -6 to 6
- query_matrix: bfloat16 [1024, 1024], P(('dp', 'seq')), may hold values from -0.1875 to 0.1875
- key_matrix: bfloat16 [1024, 512], P(('dp', 'seq')), may hold values from -0.1875 to 0.1875
- value_matrix: bfloat16 [1024, 512], P(('dp', 'seq')), may hold values from -0.1875 to 0.1875
- output_matrix: bfloat16 [1024, 1024], P(('dp', 'seq')), may hold values from -2 to 2
- attention_gain: bfloat16 [1024], P(('dp', 'seq')), may hold values from 0.5 to 1.5
- expert_gain: bfloat16 [1024], P(('dp', 'seq')), may hold values from 0.5 to 1.5
- router_matrix: bfloat16 [1024, 16], P(('dp', 'seq')), may hold values from -0.09375 to 0.09375
- gate_up_weight: bfloat16 [1024, 16, 1024], P(('dp', 'seq')), may hold values from -0.1875 to 0.1875
- down_weight: bfloat16 [1024, 16, 512], P(('dp', 'seq')), may hold values from -2 to 2
Outputs:
- mixed: bfloat16 [8, 512, 1024], P('dp', 'seq')
- tokens_grad: float32 [8, 512, 1024], P('dp', 'seq')
- query_weight_grad: float32 [1024, 1024], P(('dp', 'seq'))
- key_weight_grad: float32 [1024, 512], P(('dp', 'seq'))
- value_weight_grad: float32 [1024, 512], P(('dp', 'seq'))
- output_weight_grad: float32 [1024, 1024], P(('dp', 'seq'))
- attention_gain_grad: float32 [1024], P(('dp', 'seq'))
- expert_gain_grad: float32 [1024], P(('dp', 'seq'))
- router_weight_grad: float32 [1024, 16], P(('dp', 'seq'))
- gate_up_weight_grad: float32 [1024, 16, 1024], P(('dp', 'seq'))
- down_weight_grad: float32 [1024, 16, 512], P(('dp', 'seq'))
Inputs may be any that keep to these rules, and one draw needn't show every extreme that they name: `routes`: each token names 8 different experts. Among the 128 rows of one device no expert is named by more than 96 tokens, and in some device one expert is named by exactly 96.
All inputs are finite; a program needn't handle non-finite values.
Results may differ from a plain program's by a relative error of at most 0.02.
Values may be sent and summed in bfloat16 or wider, within the bound.
A program may use at most 384 MiB of HBM per device.

v0:
```python
import math

import jax
import jax.numpy as jnp
from jax import lax
from jax.sharding import PartitionSpec as P

HEAD_WIDTH = 64
CAPACITY = 96


NORM_EPS = 1e-06
LOW_SCORE = -1e30


def rotary_tables(positions, head_dim):
    half_dim = head_dim // 2
    frequency = jnp.exp(
        jnp.arange(half_dim, dtype=jnp.float32) * (-2.0 * math.log(10000.0) / head_dim)
    )
    angles = positions.astype(jnp.float32)[:, None] * frequency[None, :]
    return (jnp.cos(angles), jnp.sin(angles))


def rotate(value_rows, cosine, sine_table):
    half_dim = value_rows.shape[-1] // 2
    first_half = value_rows[..., :half_dim]
    second = value_rows[..., half_dim:]
    cos_heads = cosine[:, None, :]
    sin_heads = sine_table[:, None, :]
    return jnp.concatenate(
        [first_half * cos_heads - second * sin_heads, second * cos_heads + first_half * sin_heads],
        axis=-1,
    )


def norm_back(grad_normed, normed, inverse):
    return inverse * (grad_normed - normed * jnp.mean(grad_normed * normed, -1, keepdims=True))


def keep_state(running):
    return running


def swiglu(mid_linear, ff_width):
    return (jax.nn.silu(mid_linear[..., :ff_width]) * mid_linear[..., ff_width:]).astype(
        jnp.bfloat16
    )


def swiglu_back(act_grad, mid_linear, ff_width):
    gate_part = mid_linear[..., :ff_width]
    up_part = mid_linear[..., ff_width:]
    sigmoid = jax.nn.sigmoid(gate_part)
    gate_slope = sigmoid * (1.0 + gate_part * (1.0 - sigmoid))
    return jnp.concatenate(
        [act_grad * up_part * gate_slope, act_grad * gate_part * sigmoid], axis=-1
    ).astype(jnp.bfloat16)


def over_key_blocks(pieces, block_fn, running):
    piece_rows = pieces[0].shape[0]
    block_size = math.gcd(piece_rows, 512)
    shaped = tuple(
        (piece.reshape(piece_rows // block_size, block_size, piece.shape[1]) for piece in pieces)
    )
    offsets = block_size * jnp.arange(piece_rows // block_size, dtype=jnp.int32)

    def advance(carried, block_item):
        return (block_fn(carried, block_item[0], block_item[1], block_item[2]), None)

    result_state, unused = lax.scan(advance, running, (shaped[0], shaped[1], offsets))
    return result_state


def per_device(
    tokens,
    prefix_len,
    routes,
    cotangent,
    query_matrix,
    key_matrix,
    value_matrix,
    output_matrix,
    attention_gain,
    expert_gain,
    router_matrix,
    gate_up_weight,
    down_weight,
):
    hidden = tokens[0].astype(jnp.float32)
    tok_rows, model_width = hidden.shape
    params = (
        lax.all_gather(query_matrix, ("dp", "seq"), axis=0, tiled=True),
        lax.all_gather(key_matrix, ("dp", "seq"), axis=0, tiled=True),
        lax.all_gather(value_matrix, ("dp", "seq"), axis=0, tiled=True),
        lax.all_gather(output_matrix, ("dp", "seq"), axis=0, tiled=True),
        lax.all_gather(attention_gain, ("dp", "seq"), axis=0, tiled=True),
        lax.all_gather(expert_gain, ("dp", "seq"), axis=0, tiled=True),
        lax.all_gather(router_matrix, ("dp", "seq"), axis=0, tiled=True),
    )
    query_full, key_full, value_full, output_full, gain_attention, gain_expert, router_full = params
    head_dim = HEAD_WIDTH
    query_width = query_full.shape[1]
    key_width = key_full.shape[1]
    query_heads = query_width // head_dim
    key_groups = key_width // head_dim
    head_group = query_heads // key_groups
    score_scale = head_dim ** (-0.5)
    first_place = lax.axis_index("seq") * tok_rows
    positions = first_place + jnp.arange(tok_rows, dtype=jnp.int32)
    last_place = first_place + tok_rows - 1
    prefix_end = prefix_len[0]
    cosine, sine_table = rotary_tables(positions, head_dim)
    inverse_attention = lax.rsqrt(jnp.mean(hidden * hidden, -1, keepdims=True) + NORM_EPS)
    normed_attention = hidden * inverse_attention
    attention_input = (normed_attention * gain_attention.astype(jnp.float32)).astype(jnp.bfloat16)
    query_projected = jnp.dot(
        attention_input, query_full, preferred_element_type=jnp.float32
    ).reshape(tok_rows, query_heads, head_dim)
    queries = (
        rotate(query_projected, cosine, sine_table)
        .astype(jnp.bfloat16)
        .reshape(tok_rows, key_groups, head_group, head_dim)
    )
    key_projected = jnp.dot(attention_input, key_full, preferred_element_type=jnp.float32).reshape(
        tok_rows, key_groups, head_dim
    )
    keys_local = (
        rotate(key_projected, cosine, sine_table).astype(jnp.bfloat16).reshape(tok_rows, key_width)
    )
    values_local = jnp.dot(attention_input, value_full, preferred_element_type=jnp.float32).astype(
        jnp.bfloat16
    )

    def block_scores(key_block, key_start):
        block_size = key_block.shape[0]
        key_heads = key_block.reshape(block_size, key_groups, head_dim)
        key_places = key_start + jnp.arange(block_size, dtype=jnp.int32)
        allowed = (key_places[None, :] <= positions[:, None]) | (key_places[None, :] < prefix_end)
        scores = (
            jnp.einsum("qhgd,khd->hgqk", queries, key_heads, preferred_element_type=jnp.float32)
            * score_scale
        )
        return (jnp.where(allowed, scores, -jnp.inf), key_heads)

    def attend(running, key_block, value_block, key_start):

        def compute(carried):
            run_max, run_sum, weighted = carried
            scores, key_heads = block_scores(key_block, key_start)
            value_heads = value_block.reshape(key_block.shape[0], key_groups, head_dim)
            new_max = jnp.maximum(run_max, jnp.max(scores, -1))
            weights = jnp.exp(scores - new_max[..., None])
            factor = jnp.exp(run_max - new_max)
            new_sum = run_sum * factor + jnp.sum(weights, -1)
            new_weighted = weighted * factor[..., None] + jnp.einsum(
                "hgqk,khd->hgqd",
                weights.astype(jnp.bfloat16),
                value_heads,
                preferred_element_type=jnp.float32,
            )
            return (new_max, new_sum, new_weighted)

        visible = (key_start <= last_place) | (key_start < prefix_end)
        return lax.cond(visible, compute, keep_state, running)

    stat_shape = (key_groups, head_group, tok_rows)
    start_state = (
        jnp.full(stat_shape, LOW_SCORE, jnp.float32),
        jnp.zeros(stat_shape, jnp.float32),
        jnp.zeros(stat_shape + (head_dim,), jnp.float32),
    )
    run_max, run_sum, weighted = over_key_blocks(
        (
            lax.all_gather(keys_local, "seq", axis=0, tiled=True),
            lax.all_gather(values_local, "seq", axis=0, tiled=True),
        ),
        attend,
        start_state,
    )
    log_total = run_max + jnp.log(run_sum)
    attended_heads = weighted / run_sum[..., None]
    attention_lowered = (
        attended_heads.transpose(2, 0, 1, 3).reshape(tok_rows, query_width).astype(jnp.bfloat16)
    )
    branch_output = jnp.einsum(
        "tc,dc->td", attention_lowered, output_full, preferred_element_type=jnp.float32
    )
    middle = hidden + branch_output
    inverse_expert = lax.rsqrt(jnp.mean(middle * middle, -1, keepdims=True) + NORM_EPS)
    normed_expert = middle * inverse_expert
    expert_input = (normed_expert * gain_expert.astype(jnp.float32)).astype(jnp.bfloat16)
    router_logits = jnp.dot(expert_input, router_full, preferred_element_type=jnp.float32)
    router_probs = jax.nn.softmax(router_logits, axis=-1)
    expert_count = router_full.shape[1]
    route_ids = routes[0]
    expert_range = jnp.arange(expert_count, dtype=jnp.int32)
    route_hits = jnp.sum(
        (route_ids[:, :, None] == expert_range[None, None, :]).astype(jnp.int32), 1
    )
    slot_rank = jnp.cumsum(route_hits, 0) - 1
    slot_target = jnp.where(route_hits > 0, slot_rank, CAPACITY)
    token_index = jnp.broadcast_to(
        jnp.arange(tok_rows, dtype=jnp.int32)[:, None], (tok_rows, expert_count)
    )
    expert_index = jnp.broadcast_to(expert_range[None, :], (tok_rows, expert_count))
    slot_table = (
        jnp.zeros((expert_count, CAPACITY), jnp.int32)
        .at[expert_index, slot_target]
        .set(token_index, mode="drop")
    )
    slot_live = jnp.arange(CAPACITY, dtype=jnp.int32)[None, :] < jnp.sum(route_hits, 0)[:, None]
    expert_column = expert_range[:, None]
    dispatched = expert_input[slot_table]
    slot_gates = jnp.where(slot_live, router_probs[slot_table, expert_column], 0.0)
    ff_width = down_weight.shape[2]
    grad_mid = cotangent[0].astype(jnp.float32)
    slot_grad = grad_mid[slot_table]
    out_grad = (slot_gates[..., None] * slot_grad).astype(jnp.bfloat16)
    gate_up_full, down_full = (
        lax.all_gather(gate_up_weight, ("dp", "seq"), axis=0, tiled=True),
        lax.all_gather(down_weight, ("dp", "seq"), axis=0, tiled=True),
    )
    mid_linear = jnp.einsum(
        "ecd,def->ecf", dispatched, gate_up_full, preferred_element_type=jnp.float32
    )
    activation = swiglu(mid_linear, ff_width)
    expert_out = jnp.einsum(
        "ecf,def->ecd", activation, down_full, preferred_element_type=jnp.float32
    )
    flat_slots = slot_table.reshape(-1)
    combined = (
        jnp.zeros((tok_rows, model_width), jnp.float32)
        .at[flat_slots]
        .add((slot_gates[..., None] * expert_out).reshape(-1, model_width))
    )
    mixed = (middle + combined).astype(jnp.bfloat16)
    gate_grad = jnp.where(slot_live, jnp.sum(expert_out * slot_grad, -1), 0.0)
    act_grad = jnp.einsum("ecd,def->ecf", out_grad, down_full, preferred_element_type=jnp.float32)
    mid_grad = swiglu_back(act_grad, mid_linear, ff_width)
    gate_up_term = jnp.einsum(
        "ecd,ecf->def", dispatched, mid_grad, preferred_element_type=jnp.float32
    )
    down_term = jnp.einsum("ecd,ecf->def", out_grad, activation, preferred_element_type=jnp.float32)
    summed_terms = lax.psum_scatter(
        jnp.concatenate([gate_up_term, down_term], axis=-1),
        ("dp", "seq"),
        scatter_dimension=0,
        tiled=True,
    )
    gate_up_weight_grad = summed_terms[..., : 2 * ff_width]
    down_weight_grad = summed_terms[..., 2 * ff_width :]
    dispatched_grad = jnp.einsum(
        "ecf,def->ecd", mid_grad, gate_up_full, preferred_element_type=jnp.float32
    )
    expert_in_grad = (
        jnp.zeros((tok_rows, model_width), jnp.float32)
        .at[flat_slots]
        .add(dispatched_grad.reshape(-1, model_width))
    )
    prob_grad = (
        jnp.zeros((tok_rows, expert_count), jnp.float32)
        .at[slot_table, expert_column]
        .add(gate_grad)
    )
    logit_grad = (
        router_probs * (prob_grad - jnp.sum(router_probs * prob_grad, -1, keepdims=True))
    ).astype(jnp.bfloat16)
    router_term = jnp.einsum(
        "td,te->de", expert_input, logit_grad, preferred_element_type=jnp.float32
    )
    expert_in_grad = expert_in_grad + jnp.einsum(
        "te,de->td", logit_grad, router_full, preferred_element_type=jnp.float32
    )
    expert_gain_term = jnp.sum(expert_in_grad * normed_expert, 0)
    grad_res = grad_mid + norm_back(
        expert_in_grad * gain_expert.astype(jnp.float32), normed_expert, inverse_expert
    )
    branch_grad = grad_res.astype(jnp.bfloat16)
    output_term = jnp.einsum(
        "td,tc->dc", branch_grad, attention_lowered, preferred_element_type=jnp.float32
    )
    attended_grad = jnp.dot(branch_grad, output_full, preferred_element_type=jnp.float32).astype(
        jnp.bfloat16
    )
    attended_grad_heads = attended_grad.reshape(
        tok_rows, key_groups, head_group, head_dim
    ).transpose(1, 2, 0, 3)
    delta = jnp.sum(attended_grad_heads.astype(jnp.float32) * attended_heads, -1)
    seq_total = tok_rows * lax.axis_size("seq")

    def attend_back(running, key_block, value_block, key_start):

        def compute(carried):
            query_sum, key_sum, value_sum = carried
            block_size = key_block.shape[0]
            scores, key_heads = block_scores(key_block, key_start)
            value_heads = value_block.reshape(block_size, key_groups, head_dim)
            probs_full = jnp.exp(scores - log_total[..., None])
            probs_low = probs_full.astype(jnp.bfloat16)
            value_piece = jnp.einsum(
                "hgqk,hgqd->khd", probs_low, attended_grad_heads, preferred_element_type=jnp.float32
            ).reshape(block_size, key_width)
            prob_part = jnp.einsum(
                "hgqd,khd->hgqk",
                attended_grad_heads,
                value_heads,
                preferred_element_type=jnp.float32,
            )
            score_grad = (probs_full * (prob_part - delta[..., None])).astype(jnp.bfloat16)
            query_sum = (
                query_sum
                + jnp.einsum(
                    "hgqk,khd->hgqd", score_grad, key_heads, preferred_element_type=jnp.float32
                )
                * score_scale
            )
            key_piece = (
                jnp.einsum(
                    "hgqk,qhgd->khd", score_grad, queries, preferred_element_type=jnp.float32
                )
                * score_scale
            ).reshape(block_size, key_width)
            key_sum = lax.dynamic_update_slice_in_dim(
                key_sum,
                lax.dynamic_slice_in_dim(key_sum, key_start, block_size, 0) + key_piece,
                key_start,
                0,
            )
            value_sum = lax.dynamic_update_slice_in_dim(
                value_sum,
                lax.dynamic_slice_in_dim(value_sum, key_start, block_size, 0) + value_piece,
                key_start,
                0,
            )
            return (query_sum, key_sum, value_sum)

        visible = (key_start <= last_place) | (key_start < prefix_end)
        return lax.cond(visible, compute, keep_state, running)

    back_start = (
        jnp.zeros(stat_shape + (head_dim,), jnp.float32),
        jnp.zeros((seq_total, key_width), jnp.float32),
        jnp.zeros((seq_total, key_width), jnp.float32),
    )
    query_sum, key_sum, value_sum = over_key_blocks(
        (
            lax.all_gather(keys_local, "seq", axis=0, tiled=True),
            lax.all_gather(values_local, "seq", axis=0, tiled=True),
        ),
        attend_back,
        back_start,
    )
    key_part, value_part = (
        lax.psum_scatter(
            key_sum.astype(jnp.bfloat16), "seq", scatter_dimension=0, tiled=True
        ).astype(jnp.float32),
        lax.psum_scatter(
            value_sum.astype(jnp.bfloat16), "seq", scatter_dimension=0, tiled=True
        ).astype(jnp.float32),
    )
    query_rows = query_sum.transpose(2, 0, 1, 3).reshape(tok_rows, query_heads, head_dim)
    query_grad = (
        rotate(query_rows, cosine, -sine_table).reshape(tok_rows, query_width).astype(jnp.bfloat16)
    )
    key_grad = (
        rotate(key_part.reshape(tok_rows, key_groups, head_dim), cosine, -sine_table)
        .reshape(tok_rows, key_width)
        .astype(jnp.bfloat16)
    )
    value_grad = value_part.astype(jnp.bfloat16)
    query_term = jnp.einsum(
        "td,tc->dc", attention_input, query_grad, preferred_element_type=jnp.float32
    )
    key_term = jnp.einsum(
        "td,tc->dc", attention_input, key_grad, preferred_element_type=jnp.float32
    )
    value_term = jnp.einsum(
        "td,tc->dc", attention_input, value_grad, preferred_element_type=jnp.float32
    )
    attention_in_grad = jnp.einsum(
        "tc,dc->td", query_grad, query_full, preferred_element_type=jnp.float32
    )
    attention_in_grad = attention_in_grad + jnp.einsum(
        "tc,dc->td", key_grad, key_full, preferred_element_type=jnp.float32
    )
    attention_in_grad = attention_in_grad + jnp.einsum(
        "tc,dc->td", value_grad, value_full, preferred_element_type=jnp.float32
    )
    attention_gain_term = jnp.sum(attention_in_grad * normed_attention, 0)
    tokens_grad = grad_res + norm_back(
        attention_in_grad * gain_attention.astype(jnp.float32), normed_attention, inverse_attention
    )
    summed_grads = (
        lax.psum_scatter(query_term, ("dp", "seq"), scatter_dimension=0, tiled=True),
        lax.psum_scatter(key_term, ("dp", "seq"), scatter_dimension=0, tiled=True),
        lax.psum_scatter(value_term, ("dp", "seq"), scatter_dimension=0, tiled=True),
        lax.psum_scatter(output_term, ("dp", "seq"), scatter_dimension=0, tiled=True),
        lax.psum_scatter(attention_gain_term, ("dp", "seq"), scatter_dimension=0, tiled=True),
        lax.psum_scatter(expert_gain_term, ("dp", "seq"), scatter_dimension=0, tiled=True),
        lax.psum_scatter(router_term, ("dp", "seq"), scatter_dimension=0, tiled=True),
    )
    return (
        mixed[None],
        tokens_grad[None],
        summed_grads[0],
        summed_grads[1],
        summed_grads[2],
        summed_grads[3],
        summed_grads[4],
        summed_grads[5],
        summed_grads[6],
        gate_up_weight_grad,
        down_weight_grad,
    )


def solution(mesh):
    return jax.shard_map(
        per_device,
        mesh=mesh,
        in_specs=(
            P("dp", "seq", None),
            P("dp"),
            P("dp", "seq", None),
            P("dp", "seq", None),
            P(("dp", "seq"), None),
            P(("dp", "seq"), None),
            P(("dp", "seq"), None),
            P(("dp", "seq"), None),
            P(("dp", "seq")),
            P(("dp", "seq")),
            P(("dp", "seq"), None),
            P(("dp", "seq"), None, None),
            P(("dp", "seq"), None, None),
        ),
        out_specs=(
            P("dp", "seq", None),
            P("dp", "seq", None),
            P(("dp", "seq"), None),
            P(("dp", "seq"), None),
            P(("dp", "seq"), None),
            P(("dp", "seq"), None),
            P(("dp", "seq")),
            P(("dp", "seq")),
            P(("dp", "seq"), None),
            P(("dp", "seq"), None, None),
            P(("dp", "seq"), None, None),
        ),
        check_vma=False,
    )
```

profile of v0, /device:TPU:0, one launch (start us, length us, event | category | flops | bytes accessed | tf_op | source)
XLA Modules:
  0.0 2287.0 jit_solution(13558922433173180874)
XLA Ops:
  16.3 42.0 %all-reduce.5 = (bf16[1024]{0:T(1024)(128)(2,1)S(1)}, bf16[1024]{0:T(1024)(128)(2,1)S(1)}) all-reduce(bf16[1024]{0:T(1024)(128)(2,1)S(1)} %dynamic-update-slice, bf16[1024]{0:T(1024)(128)(2,1)S(1)} %dynamic-update-slice.1), channel_id=1, replica_groups=mesh['dp'=8,'seq'=4] {'dp','seq'}, use_global_device_ids=true, to_apply=%add | all-reduce | flops 2048 | bytes 8192
  58.4 67.3 %all-gather = bf16[32,32,16]{1,2,0:T(8,128)(2,1)S(1)} all-gather(bf16[1,32,16]{1,2,0:T(8,128)(2,1)S(1)} %bitcast.253), channel_id=1, replica_groups=mesh['dp'=8,'seq'=4] {'dp','seq'}, dimensions={0}, use_global_device_ids=true | all-gather | bytes 33792 | tf_op jit(solution)/shard_map/all_gather | solution.py:100
  126.6 23.3 %fusion.84 = s32[128,16,1]{2,1,0:T(8,128)S(1)} fusion(s32[128,16,1]{2,1,0:T(8,128)S(1)} %copy.114), kind=kOutput, calls=%fused_computation.163 | output fusion | flops 260096 | bytes 16384 | tf_op jit(solution)/shard_map/jit(cumsum)/reduce_window_sum | solution.py:202
  172.5 17.0 all_gather.40
  189.5 14.3 all_gather.37
  217.0 25.5 %all-gather.14.cloned.1.call-done = bf16[1024,1024]{1,0:T(8,128)(2,1)} async-done(((bf16[32,1024]{1,0:T(8,128)(2,1)}), bf16[1024,1024]{1,0:T(8,128)(2,1)}) %all-gather.14.cloned.1.call-update) | async-done | bytes 2097168 | tf_op jit(solution)/shard_map/all_gather | solution.py:97
  251.2 187.7 %all-gather.16.cloned.1.call-done = bf16[1024,16,1024]{2,0,1:T(8,128)(2,1)} async-done(((bf16[32,16,1024]{2,0,1:T(8,128)(2,1)}), bf16[1024,16,1024]{2,0,1:T(8,128)(2,1)}) %all-gather.16.cloned.1.call-update) | async-done | bytes 33554448 | tf_op jit(solution)/shard_map/all_gather | solution.py:222
  438.9 19.9 fusion.85
  462.7 93.4 %all-gather.18.cloned.1.call-done = bf16[1024,16,512]{2,0,1:T(8,128)(2,1)} async-done(((bf16[32,16,512]{2,0,1:T(8,128)(2,1)}), bf16[1024,16,512]{2,0,1:T(8,128)(2,1)}) %all-gather.18.cloned.1.call-update) | async-done | bytes 16777232 | tf_op jit(solution)/shard_map/all_gather | solution.py:223
  590.2 13.0 multiply_convert_fusion.3
  603.2 18.8 fusion.26
  622.0 14.9 scatter_fusion.1
  646.1 17.8 conditional.3
  666.3 25.9 %convolution_bitcast_fusion.1 = f32[1024,16,1024]{0,2,1:T(8,128)} fusion(bf16[16,96,1024]{2,1,0:T(8,128)(2,1)} %bitcast.220, bf16[16,96,512]{2,1,0:T(8,128)(2,1)} %copy-done.13, bf16[16,96,512]{2,1,0:T(8,128)(2,1)} %copy-done.12), kind=kOutput, calls=%fused_computation.45 | convolution fusion | flops 3227516928 | bytes 73400320 | tf_op jit(solution)/shard_map/ecd,ecf->def/dot_general | solution.py:242
  694.5 16.0 convolution_bitcast_fusion.2
  710.8 66.8 %pad_maximum_fusion = f32[1024,16,1536]{0,2,1:T(8,128)} fusion(f32[1024,16,512]{0,2,1:T(8,128)} %convolution_bitcast_fusion.2, f32[1024,16,1024]{0,2,1:T(8,128)} %convolution_bitcast_fusion.1), kind=kLoop, calls=%fused_computation.44 | loop fusion | flops 25165824 | bytes 201326592 | tf_op jit(solution)/shard_map/concatenate | solution.py:247
  777.6 99.9 %copy.127 = f32[1024,16,1536]{2,1,0:T(8,128)} copy(f32[1024,16,1536]{0,2,1:T(8,128)} %pad_maximum_fusion) | data formatting | bytes 201326592 | tf_op jit(solution)/shard_map/concatenate | solution.py:247
  900.2 15.4 scatter_fusion
  923.6 38.7 %all-reduce.4 = (f32[1024]{0:T(1024)S(1)}, f32[1024]{0:T(1024)S(1)}) all-reduce(f32[1024]{0:T(1024)S(1)} %get-tuple-element.305, f32[1024]{0:T(1024)S(1)} %copy-done.29), channel_id=8, replica_groups=mesh['dp'=8,'seq'=4] {'dp','seq'}, use_global_device_ids=true, to_apply=%region_29.30.clone | all-reduce | flops 2048 | bytes 16384
  964.5 738.3 %reduce-scatter.23.cloned.1.call-done = f32[32,16,1536]{2,1,0:T(8,128)} async-done(((f32[1024,16,1536]{2,1,0:T(8,128)}), f32[32,16,1536]{2,1,0:T(8,128)}) %reduce-scatter.23.cloned.1.call-update) | async-done | bytes 3145744 | tf_op jit(solution)/shard_map/reduce_scatter | solution.py:246
  1708.2 134.8 %reduce-scatter.19.cloned.1.call-done = f32[32,512]{1,0:T(8,128)} async-done(((f32[1024,512]{1,0:T(8,128)}), f32[32,512]{1,0:T(8,128)}) %reduce-scatter.19.cloned.1.call-update) | async-done | bytes 65552 | tf_op jit(solution)/shard_map/reduce_scatter | solution.py:398
  1843.0 138.5 %reduce-scatter.17.cloned.1.call-done = f32[32,512]{1,0:T(8,128)} async-done(((f32[1024,512]{1,0:T(8,128)}), f32[32,512]{1,0:T(8,128)}) %reduce-scatter.17.cloned.1.call-update) | async-done | bytes 65552 | tf_op jit(solution)/shard_map/reduce_scatter | solution.py:397
  1981.5 149.0 %reduce-scatter.21.cloned.1.call-done = f32[32,1024]{1,0:T(8,128)} async-done(((f32[1024,1024]{1,0:T(8,128)}), f32[32,1024]{1,0:T(8,128)}) %reduce-scatter.21.cloned.1.call-update) | async-done | bytes 131088 | tf_op jit(solution)/shard_map/reduce_scatter | solution.py:399
  2130.6 149.4 %reduce-scatter.15.cloned.1.call-done = f32[32,1024]{1,0:T(8,128)} async-done(((f32[1024,1024]{1,0:T(8,128)}), f32[32,1024]{1,0:T(8,128)}) %reduce-scatter.15.cloned.1.call-update) | async-done | bytes 131088 | tf_op jit(solution)/shard_map/reduce_scatter | solution.py:396
  (244 shorter events, 166.0 us)
Async XLA Ops:
  7.2 51.2 %copy-start.30 = (bf16[32,16]{0,1:T(8,128)(2,1)S(1)}, bf16[32,16]{0,1:T(8,128)(2,1)}, u32[]{:S(2)}) copy-start(bf16[32,16]{0,1:T(8,128)(2,1)} %param.27) | copy-start | bytes 3076
  7.2 118.8 %copy-start.31 = (s32[1,128,8]{1,2,0:T(8,128)S(1)}, s32[1,128,8]{1,2,0:T(8,128)}, u32[]{:S(2)}) copy-start(s32[1,128,8]{1,2,0:T(8,128)} %param.19) | copy-start | bytes 12292
  7.2 161.6 %all-gather.8.cloned.1.call-start = ((), (), s32[]{:S(2)}) async-start(), calls=%async_computation.8 | async-start | bytes 1081344 | tf_op jit(solution)/shard_map/all_gather | solution.py:95
  8.0 162.9 %all-gather.12.cloned.1.call-start = ((), (), s32[]{:S(2)}) async-start(), calls=%async_computation.10 | async-start | bytes 1081344 | tf_op jit(solution)/shard_map/all_gather | solution.py:96
  8.7 195.1 %all-gather.10.cloned.1.call-start = ((), (), s32[]{:S(2)}) async-start(), calls=%async_computation.9 | async-start | bytes 2162688 | tf_op jit(solution)/shard_map/all_gather | solution.py:94
  9.4 233.1 %all-gather.14.cloned.1.call-start = ((), (), s32[]{:S(2)}) async-start(), calls=%async_computation.11 | async-start | bytes 2162688 | tf_op jit(solution)/shard_map/all_gather | solution.py:97
  10.0 428.9 %all-gather.16.cloned.1.call-start = ((), (), s32[]{:S(2)}) async-start(), calls=%async_computation.12 | async-start | bytes 34603008 | tf_op jit(solution)/shard_map/all_gather | solution.py:222
  12.9 543.2 %all-gather.18.cloned.1.call-start = ((), (), s32[]{:S(2)}) async-start(), calls=%async_computation.13 | async-start | bytes 17301504 | tf_op jit(solution)/shard_map/all_gather | solution.py:223
  15.1 862.5 %reduce-scatter.27.cloned.1.call-start = ((), (), s32[]{:S(2)}) async-start(), calls=%async_computation.20 | async-start | bytes 655360
  58.3 149.4 %copy-start.23 = (f32[1024]{0:T(1024)}, f32[1024]{0:T(1024)S(1)}, u32[]{:S(2)}) copy-start(f32[1024]{0:T(1024)S(1)} %convert_element_type.145) | copy-start | bytes 12292
  160.8 50.2 %copy-start.7 = (f32[8,2,128,64]{2,3,1,0:T(8,128)}, f32[8,2,128,64]{2,3,1,0:T(8,128)S(1)}, u32[]{:S(2)}) copy-start(f32[8,2,128,64]{2,3,1,0:T(8,128)S(1)} %broadcast.291) | copy-start | bytes 1572868
  167.8 454.2 %copy-start.26 = (s32[1536]{0:T(1024)}, s32[1536]{0:T(1024)S(1)}, u32[]{:S(2)}) copy-start(s32[1536]{0:T(1024)S(1)} %fusion.65) | copy-start | bytes 18436
  168.0 39.7 %copy-start.27 = (f32[128]{0:T(128)}, f32[128]{0:T(128)S(1)}, u32[]{:S(2)}) copy-start(f32[128]{0:T(128)S(1)} %add_rsqrt_fusion.1) | copy-start | bytes 1540
  168.8 41.3 %copy-start.21 = (f32[128,32]{0,1:T(8,128)}, f32[128,32]{0,1:T(8,128)S(1)}, u32[]{:S(2)}) copy-start(f32[128,32]{0,1:T(8,128)S(1)} %get-tuple-element.340) | copy-start | bytes 49156
  189.5 21.4 copy-start.14
  217.0 28.0 %copy-start.15 = (bf16[8,2,128,64]{2,3,1,0:T(8,128)(2,1)}, bf16[8,2,128,64]{2,3,1,0:T(8,128)(2,1)S(1)}, u32[]{:S(2)}) copy-start(bf16[8,2,128,64]{2,3,1,0:T(8,128)(2,1)S(1)} %get-tuple-element.320) | copy-start | bytes 786436
  245.0 392.7 %copy-start = (f32[128,1024]{1,0:T(8,128)}, f32[128,1024]{1,0:T(8,128)S(1)}, u32[]{:S(2)}) copy-start(f32[128,1024]{1,0:T(8,128)S(1)} %get-tuple-element.342) | copy-start | bytes 1572868
  666.3 215.0 %reduce-scatter.25.cloned.1.call-start = ((), (), s32[]{:S(2)}) async-start(), calls=%async_computation.19 | async-start | bytes 655360
  694.4 223.9 %reduce-scatter.29.cloned.1.call-start = ((), (), s32[]{:S(2)}) async-start(), calls=%async_computation.21 | async-start | bytes 540672
  710.5 992.3 %reduce-scatter.23.cloned.1.call-start = ((), (), s32[]{:S(2)}) async-start(), calls=%async_computation.18 | async-start | bytes 103809024 | tf_op jit(solution)/shard_map/reduce_scatter | solution.py:246
  877.5 965.5 %reduce-scatter.19.cloned.1.call-start = ((), (), s32[]{:S(2)}) async-start(), calls=%async_computation.16 | async-start | bytes 2162688 | tf_op jit(solution)/shard_map/reduce_scatter | solution.py:398
  881.2 1100.3 %reduce-scatter.17.cloned.1.call-start = ((), (), s32[]{:S(2)}) async-start(), calls=%async_computation.15 | async-start | bytes 2162688 | tf_op jit(solution)/shard_map/reduce_scatter | solution.py:397
  884.6 1246.0 %reduce-scatter.21.cloned.1.call-start = ((), (), s32[]{:S(2)}) async-start(), calls=%async_computation.17 | async-start | bytes 4325376 | tf_op jit(solution)/shard_map/reduce_scatter | solution.py:399
  887.9 1392.1 %reduce-scatter.15.cloned.1.call-start = ((), (), s32[]{:S(2)}) async-start(), calls=%async_computation.14 | async-start | bytes 4325376 | tf_op jit(solution)/shard_map/reduce_scatter | solution.py:396
  (28 other events, 171.1 us)
Sparse Core Ops, SparseCore 0:
  11.0 56.5 all-gather.7
  70.6 52.8 all-gather.11
  126.4 56.4 all-gather.9
  185.7 56.7 all-gather.13
  245.9 192.9 all-gather.15
  441.8 114.1 all-gather.17
  666.4 19.9 reduce-scatter.26
  694.5 20.0 reduce-scatter.24
  717.5 132.7 reduce-scatter.28
  877.6 825.0 reduce-scatter.22
  1705.7 137.2 reduce-scatter.18
  1845.7 135.7 reduce-scatter.16
  1984.5 146.0 reduce-scatter.20
  2133.4 146.5 reduce-scatter.14
where the time goes:
time: 2300 us; the launch traced here: 2290 us
  waiting for transfers between devices  1620 us (70%)
  blocking collectives  179 us (8%)
  local copies, waits for them, and re-layouts  167 us (7%)
  other arithmetic  161 us (7%)
  matrix products  143 us (6%)
    reduce_scatter x1, waiting for transfers between devices, per_device(): lax.psum_scatter(jnp.concatenate([gate_up_term, down_term], axis=-1), ('d...  738 us
    all_gather x1, waiting for transfers between devices, per_device(): lax.all_gather(gate_up_weight, ('dp', 'seq'), axis=0, tiled=True)  188 us
    reduce_scatter x1, waiting for transfers between devices, per_device(): lax.psum_scatter(query_term, ('dp', 'seq'), scatter_dimension=0, tiled=True)  149 us
    reduce_scatter x1, waiting for transfers between devices, per_device(): lax.psum_scatter(output_term, ('dp', 'seq'), scatter_dimension=0, tiled=T...  149 us
    reduce_scatter x1, waiting for transfers between devices, per_device(): lax.psum_scatter(key_term, ('dp', 'seq'), scatter_dimension=0, tiled=True)  139 us
    reduce_scatter x1, waiting for transfers between devices, per_device(): lax.psum_scatter(value_term, ('dp', 'seq'), scatter_dimension=0, tiled=True)  135 us
    concatenate x1, local copies, waits for them, and re-layouts, per_device(): jnp.concatenate([gate_up_term, down_term], axis=-1)  99.9 us
    all_gather x1, waiting for transfers between devices, per_device(): lax.all_gather(down_weight, ('dp', 'seq'), axis=0, tiled=True)  93.4 us
  transfers between devices with their start and end apart: 14, of which 8 were waited for; matrix products, arithmetic and copies ran while one was open for 16% of the time, Pallas kernels for 0%

commit v1 on v0

--- a/solution.py
+++ b/solution.py
@@ -2,7 +2,10 @@
 
 import jax
 import jax.numpy as jnp
+import numpy as np
 from jax import lax
+from jax.experimental import pallas as pl
+from jax.experimental.pallas import tpu as pltpu
 from jax.sharding import PartitionSpec as P
 
 HEAD_WIDTH = 64
@@ -11,6 +14,12 @@
 
 NORM_EPS = 1e-06
 LOW_SCORE = -1e30
+LANES = 128
+HALF = HEAD_WIDTH // 2
+SCORE_SCALE = HEAD_WIDTH ** (-0.5)
+EXPERT_COUNT = 16
+KEY_HEADS = 8
+MESH = pl.DeviceIdType.MESH
 
 
 def rotary_tables(positions, head_dim):
@@ -416,9 +425,871 @@
     )
 
 
+def matmul(left, right, contract):
+    return lax.dot_general(
+        left, right, (contract, ((), ())), preferred_element_type=jnp.float32
+    )
+
+
+ROWS_BY_COLS = ((1,), (0,))
+ROWS_BY_ROWS = ((1,), (1,))
+COLS_BY_COLS = ((0,), (0,))
+
+
+def split_sum_columns(terms):
+    ones = jnp.ones((terms.shape[0], LANES), jnp.bfloat16)
+    high = terms.astype(jnp.bfloat16)
+    low = (terms - high.astype(jnp.float32)).astype(jnp.bfloat16)
+    return matmul(high, ones, COLS_BY_COLS) + matmul(low, ones, COLS_BY_COLS)
+
+
+def turned(value_rows):
+    width = value_rows.shape[1]
+    lane = lax.broadcasted_iota(jnp.int32, value_rows.shape, 1)
+    ahead = pltpu.roll(value_rows, width - HALF, 1)
+    behind = pltpu.roll(value_rows, HALF, 1)
+    return jnp.where(lane % HEAD_WIDTH < HALF, -ahead, behind)
+
+
+def spin(value_rows, cosine, sine_table):
+    repeats = value_rows.shape[1] // LANES
+    cos_all = jnp.concatenate([cosine] * repeats, 1) if repeats > 1 else cosine
+    sin_all = jnp.concatenate([sine_table] * repeats, 1) if repeats > 1 else sine_table
+    return value_rows * cos_all + turned(value_rows) * sin_all
+
+
+def shape_of(*dims, kind=jnp.bfloat16):
+    return jax.ShapeDtypeStruct(dims, kind)
+
+
+VMEM_SPEC = pl.BlockSpec(memory_space=pltpu.VMEM)
+SMEM_SPEC = pl.BlockSpec(memory_space=pltpu.SMEM)
+ANY_SPEC = pl.BlockSpec(memory_space=pl.ANY)
+
+
+class Place:
+    def __init__(self):
+        self.dp = lax.axis_index("dp")
+        self.z = lax.axis_index("seq")
+        self.lines = lax.axis_size("seq")
+        self.chips = lax.axis_size("dp") // 2
+        self.chip = self.dp // 2
+        self.core = self.dp % 2
+
+    def line_peer(self, step):
+        return (self.dp, (self.z + step) % self.lines)
+
+    def chip_peer(self, step):
+        return (((self.chip + step) % self.chips) * 2 + self.core, self.z)
+
+    def sibling(self):
+        return (self.chip * 2 + 1 - self.core, self.z)
+
+
+def meet(peers):
+    barrier = pltpu.get_barrier_semaphore()
+    for peer in peers:
+        pl.semaphore_signal(barrier, inc=1, device_id=peer, device_id_type=MESH)
+    pl.semaphore_wait(barrier, len(peers))
+
+
+def send(source, target, send_sem, recv_sem, peer):
+    copy = pltpu.make_async_remote_copy(
+        src_ref=source,
+        dst_ref=target,
+        send_sem=send_sem,
+        recv_sem=recv_sem,
+        device_id=peer,
+        device_id_type=MESH,
+    )
+    copy.start()
+    return copy
+
+
+def all_peers(here):
+    return (
+        [here.line_peer(k) for k in range(1, here.lines)]
+        + [here.chip_peer(k) for k in range(1, here.chips)]
+        + [here.sibling()]
+    )
+
+
+def comm_params(ident, limit=56):
+    return pltpu.CompilerParams(
+        collective_id=ident, has_side_effects=True, vmem_limit_bytes=limit << 20
+    )
+
+
+class Spread:
+    def __init__(self, here, pick, slot, local_sem, sends, recvs):
+        self.here, self.pick, self.slot = here, pick, slot
+        self.local_sem, self.sends, self.recvs = local_sem, sends, recvs
+
+    def start(self):
+        here = self.here
+        mine = self.slot(here.chip, here.core, here.z)
+        self.own = pltpu.make_async_copy(self.pick(here.z), mine, self.local_sem)
+        self.own.start()
+        self.line = [
+            send(
+                self.pick((here.z + k) % here.lines),
+                mine,
+                self.sends.at[k - 1],
+                self.recvs.at[k - 1],
+                here.line_peer(k),
+            )
+            for k in range(1, here.lines)
+        ]
+
+    def chips(self):
+        here = self.here
+        self.own.wait()
+        for copy in self.line:
+            copy.wait_recv()
+        mine = self.slot(here.chip, here.core, None)
+        base = here.lines - 1
+        self.plane = [
+            send(mine, mine, self.sends.at[base + k - 1], self.recvs.at[base + k - 1], here.chip_peer(k))
+            for k in range(1, here.chips)
+        ]
+        base = base + here.chips - 1
+        self.across = [send(mine, mine, self.sends.at[base], self.recvs.at[base], here.sibling())]
+
+    def cores(self):
+        here = self.here
+        base = here.lines - 1 + here.chips - 1
+        for k in range(1, here.chips):
+            self.plane[k - 1].wait_recv()
+            source = (here.chip - k + here.chips) % here.chips
+            block = self.slot(source, here.core, None)
+            self.across.append(
+                send(block, block, self.sends.at[base + k], self.recvs.at[base + k], here.sibling())
+            )
+
+    def finish(self):
+        for copy in self.across:
+            copy.wait_recv()
+        for copy in self.line + self.plane + self.across:
+            copy.wait_send()
+
+
+def spread_count(lines, chips):
+    return lines - 1 + chips - 1 + chips
+
+
+class LineGather:
+    def __init__(self, here, source, slot, local_sem, sends, recvs):
+        self.here, self.source, self.slot = here, source, slot
+        self.local_sem, self.sends, self.recvs = local_sem, sends, recvs
+
+    def start(self):
+        here = self.here
+        mine = self.slot(here.z)
+        self.own = pltpu.make_async_copy(self.source, mine, self.local_sem)
+        self.own.start()
+        self.line = [
+            send(self.source, mine, self.sends.at[k - 1], self.recvs.at[k - 1], here.line_peer(k))
+            for k in range(1, here.lines)
+        ]
+
+    def finish(self):
+        self.own.wait()
+        for copy in self.line:
+            copy.wait()
+
+
+class LineSwap:
+    def __init__(self, here, pick, received, sends, recvs):
+        self.here, self.pick, self.received = here, pick, received
+        self.sends, self.recvs = sends, recvs
+
+    def start(self):
+        here = self.here
+        self.line = [
+            send(
+                self.pick((here.z + k) % here.lines),
+                self.received(k),
+                self.sends.at[k - 1],
+                self.recvs.at[k - 1],
+                here.line_peer(k),
+            )
+            for k in range(1, here.lines)
+        ]
+
+    def finish(self):
+        for copy in self.line:
+            copy.wait()
+
+
+def front_kernel(tokens, rows, tokens_all, weights, local_sem, sends, recvs, tok_sends, tok_recvs):
+    here = Place()
+    meet(all_peers(here))
+    gather = LineGather(here, tokens, lambda z: tokens_all.at[z], local_sem.at[0], tok_sends, tok_recvs)
+
+    def slot(chip, core, z):
+        return weights.at[chip, core] if z is None else weights.at[chip, core, z]
+
+    spread = Spread(here, lambda z: rows.at[z], slot, local_sem.at[1], sends, recvs)
+    spread.start()
+    gather.start()
+    spread.chips()
+    spread.cores()
+    spread.finish()
+    gather.finish()
+
+
+def supply_kernel(
+    out_rows, expert_rows, marked, out_full, expert_full, marked_all, local_sem, o_sends, o_recvs, e_sends, e_recvs, m_sends, m_recvs
+):
+    here = Place()
+    meet(all_peers(here))
+
+    def out_slot(chip, core, z):
+        return out_full.at[chip, core] if z is None else out_full.at[chip, core, z]
+
+    def expert_slot(chip, core, z):
+        return expert_full.at[:, chip, core] if z is None else expert_full.at[:, chip, core, z]
+
+    outs = Spread(here, lambda z: out_rows, out_slot, local_sem.at[0], o_sends, o_recvs)
+    experts = Spread(here, lambda z: expert_rows.at[z], expert_slot, local_sem.at[1], e_sends, e_recvs)
+    marks = LineGather(here, marked, lambda z: marked_all.at[z], local_sem.at[2], m_sends, m_recvs)
+    outs.start()
+    experts.start()
+    marks.start()
+    outs.chips()
+    experts.chips()
+    outs.cores()
+    experts.cores()
+    outs.finish()
+    experts.finish()
+    marks.finish()
+
+
+def attend_kernel(prefix, tokens, weights, gain, cosine, sine_table, att_in, queries, keys, values, attended, attended_low, log_total):
+    rows_all, width = tokens.shape
+    qkv_width = 2 * queries.shape[1]
+    q_width, kv_width = queries.shape[1], keys.shape[1]
+    block = rows_all // lax.axis_size("seq")
+    for start in range(0, rows_all, block):
+        here = pl.ds(start, block)
+        hidden = tokens[here, :].astype(jnp.float32)
+        inverse = lax.rsqrt(jnp.mean(hidden * hidden, -1, keepdims=True) + NORM_EPS)
+        normed = (hidden * inverse * gain[...]).astype(jnp.bfloat16)
+        att_in[here, :] = normed
+        linear = matmul(normed, weights[:, :qkv_width], ROWS_BY_COLS)
+        cos_rows, sin_rows = cosine[here, :], sine_table[here, :]
+        queries[here, :] = spin(linear[:, :q_width], cos_rows, sin_rows).astype(jnp.bfloat16)
+        keys[here, :] = spin(linear[:, q_width : q_width + kv_width], cos_rows, sin_rows).astype(
+            jnp.bfloat16
+        )
+        values[here, :] = linear[:, q_width + kv_width :].astype(jnp.bfloat16)
+    prefix_end = prefix[0]
+    heads = q_width // HEAD_WIDTH
+    group = q_width // kv_width
+    for start in range(0, rows_all, block):
+        here = pl.ds(start, block)
+        reach = max(rows_all // 2, start + block)
+        query_place = start + lax.broadcasted_iota(jnp.int32, (block, reach), 0)
+        key_place = lax.broadcasted_iota(jnp.int32, (block, reach), 1)
+        allowed = (key_place <= query_place) | (key_place < prefix_end)
+        lanes = lax.broadcasted_iota(jnp.int32, (block, LANES), 1)
+        totals = jnp.zeros((block, LANES), jnp.float32)
+        outputs = []
+        for head in range(heads):
+            low = head // group * HEAD_WIDTH
+            scores = matmul(
+                queries[here, head * HEAD_WIDTH : (head + 1) * HEAD_WIDTH],
+                keys[:reach, low : low + HEAD_WIDTH],
+                ROWS_BY_ROWS,
+            )
+            scores = jnp.where(allowed, scores * SCORE_SCALE, LOW_SCORE)
+            largest = jnp.max(scores, -1, keepdims=True)
+            powers = jnp.exp(scores - largest)
+            total = jnp.sum(powers, -1, keepdims=True)
+            product = matmul(
+                powers.astype(jnp.bfloat16), values[:reach, low : low + HEAD_WIDTH], ROWS_BY_COLS
+            )
+            outputs.append(product / total)
+            totals = jnp.where(lanes == head, largest + jnp.log(total), totals)
+        joined = jnp.concatenate(outputs, 1)
+        attended[here, :] = joined
+        attended_low[here, :] = joined.astype(jnp.bfloat16)
+        log_total[here, :] = totals
+
+
+def gather_kernel(block, gathered, local_sem, sends, recvs):
+    here = Place()
+    meet([here.line_peer(k) for k in range(1, here.lines)])
+    gather = LineGather(here, block, lambda z: gathered.at[z], local_sem, sends, recvs)
+    gather.start()
+    gather.finish()
+
+
+def middle_kernel(tokens, attended_all, out_full, gain, router, expert_in, probs, middle):
+    rows_all = tokens.shape[0]
+    lines = attended_all.shape[0]
+    block = rows_all // lines
+    cols = attended_all.shape[2]
+    for start in range(0, rows_all, block):
+        here = pl.ds(start, block)
+        total = tokens[here, :].astype(jnp.float32)
+        branch = matmul(attended_all[0, here, :], out_full[:, :cols], ROWS_BY_ROWS)
+        for line in range(1, lines):
+            branch = branch + matmul(
+                attended_all[line, here, :], out_full[:, line * cols : (line + 1) * cols], ROWS_BY_ROWS
+            )
+        total = total + branch
+        inverse = lax.rsqrt(jnp.mean(total * total, -1, keepdims=True) + NORM_EPS)
+        lowered = (total * inverse * gain[...]).astype(jnp.bfloat16)
+        expert_in[here, :] = lowered
+        logits = matmul(lowered, router[...], ROWS_BY_COLS)
+        lane = lax.broadcasted_iota(jnp.int32, logits.shape, 1)
+        logits = jnp.where(lane < EXPERT_COUNT, logits, LOW_SCORE)
+        powers = jnp.exp(logits - jnp.max(logits, -1, keepdims=True))
+        powers = jnp.where(lane < EXPERT_COUNT, powers, 0.0)
+        probs[here, :] = powers / jnp.sum(powers, -1, keepdims=True)
+        middle[here, :] = total
+
+
+def expert_kernel(expert_in, marked, probs, weights, mixed_part, in_grad, gate_grad, weight_grad, mix_sum, grad_sum):
+    step = pl.program_id(0)
+    mine = lax.axis_index("seq") * pl.num_programs(0) + step
+    width = expert_in.shape[1]
+    ff_width = (weights.shape[2] - width) // 1
+    ff_width = weights.shape[2] // 3
+    half = expert_in.shape[0] // 2
+
+    @pl.when(step == 0)
+    def clear():
+        mix_sum[...] = jnp.zeros_like(mix_sum)
+        grad_sum[...] = jnp.zeros_like(grad_sum)
+        gate_grad[...] = jnp.zeros_like(gate_grad)
+
+    gate_up = weights[0, :, : 2 * ff_width]
+    down = weights[0, :, 2 * ff_width :]
+    acts, out_grads, mids = [], [], []
+    for start in (0, half):
+        here = pl.ds(start, half)
+        inputs = expert_in[here, :]
+        chosen = marked[here, width:].astype(jnp.float32)
+        lane = lax.broadcasted_iota(jnp.int32, chosen.shape, 1)
+        own = lane == mine
+        picked = jnp.sum(jnp.where(own, chosen, 0.0), -1, keepdims=True)
+        gate = jnp.sum(jnp.where(own, probs[here, :] * chosen, 0.0), -1, keepdims=True)
+        linear = matmul(inputs, gate_up, ROWS_BY_COLS)
+        gate_part, up_part = linear[:, :ff_width], linear[:, ff_width:]
+        sigmoid = 1.0 / (1.0 + jnp.exp(-gate_part))
+        silu = gate_part * sigmoid
+        act = (silu * up_part).astype(jnp.bfloat16)
+        out = matmul(act, down, ROWS_BY_ROWS)
+        grad_mid = marked[here, :width].astype(jnp.float32)
+        column = jnp.sum(out * grad_mid, -1, keepdims=True) * picked
+        gate_grad[here, :] = gate_grad[here, :] + jnp.where(own, column, 0.0)
+        mix_sum[here, :] = mix_sum[here, :] + gate * out
+        out_grad = (gate * grad_mid).astype(jnp.bfloat16)
+        act_grad = matmul(out_grad, down, ROWS_BY_COLS)
+        mid = jnp.concatenate(
+            [
+                act_grad * up_part * (sigmoid * (1.0 + gate_part * (1.0 - sigmoid))),
+                act_grad * silu,
+            ],
+            1,
+        ).astype(jnp.bfloat16)
+        grad_sum[here, :] = grad_sum[here, :] + matmul(mid, gate_up, ROWS_BY_ROWS)
+        acts.append(act)
+        out_grads.append(out_grad)
+        mids.append(mid)
+    act, out_grad, mid = (jnp.concatenate(pieces, 0) for pieces in (acts, out_grads, mids))
+    weight_grad[0, :, : 2 * ff_width] = matmul(expert_in[...], mid, COLS_BY_COLS).astype(jnp.bfloat16)
+    weight_grad[0, :, 2 * ff_width :] = matmul(out_grad, act, COLS_BY_COLS).astype(jnp.bfloat16)
+
+    @pl.when(step == pl.num_programs(0) - 1)
+    def store():
+        mixed_part[...] = mix_sum[...].astype(jnp.bfloat16)
+        in_grad[...] = grad_sum[...].astype(jnp.bfloat16)
+
+
+def settle_kernel(
+    mixed_part, in_grad, gate_grad, middle, mixed, in_total, gate_total, got_mix, got_grad, got_gate, m_sends, m_recvs, x_sends, x_recvs, g_sends, g_recvs
+):
+    here = Place()
+    meet([here.line_peer(k) for k in range(1, here.lines)])
+    swaps = [
+        LineSwap(here, lambda z: in_grad.at[z], lambda k: got_grad.at[k - 1], x_sends, x_recvs),
+        LineSwap(here, lambda z: gate_grad.at[z], lambda k: got_gate.at[k - 1], g_sends, g_recvs),
+        LineSwap(here, lambda z: mixed_part.at[z], lambda k: got_mix.at[k - 1], m_sends, m_recvs),
+    ]
+    for swap in swaps:
+        swap.start()
+    for swap in swaps:
+        swap.finish()
+    total = in_grad[here.z].astype(jnp.float32)
+    gates = gate_grad[here.z]
+    sum_mix = middle[here.z] + mixed_part[here.z].astype(jnp.float32)
+    for k in range(here.lines - 1):
+        total = total + got_grad[k].astype(jnp.float32)
+        gates = gates + got_gate[k]
+        sum_mix = sum_mix + got_mix[k].astype(jnp.float32)
+    in_total[...] = total
+    gate_total[...] = gates
+    mixed[...] = sum_mix.astype(jnp.bfloat16)
+
+
+def branch_kernel(
+    in_total, gate_total, probs, expert_in, cotangent, middle, gain, router, attended_all, out_full, grad_res, out_term, attended_grad
+):
+    z = lax.axis_index("seq")
+    lines, cols = attended_all.shape[0], attended_all.shape[3]
+    prob = probs[z]
+    gates = gate_total[...]
+    logit_grad = (prob * (gates - jnp.sum(prob * gates, -1, keepdims=True))).astype(jnp.bfloat16)
+    router_term = matmul(expert_in[z], logit_grad, COLS_BY_COLS)
+    grad = in_total[...] + matmul(logit_grad, router[...], ROWS_BY_ROWS)
+    hidden = middle[z]
+    inverse = lax.rsqrt(jnp.mean(hidden * hidden, -1, keepdims=True) + NORM_EPS)
+    normed = hidden * inverse
+    gain_term = split_sum_columns(grad * normed)
+    lane = lax.broadcasted_iota(jnp.int32, router_term.shape, 1)
+    tail = lines * cols
+    out_term[:, tail:] = jnp.where(lane == EXPERT_COUNT, gain_term, router_term).astype(jnp.bfloat16)
+    scaled = grad * gain[...]
+    result = cotangent[...].astype(jnp.float32) + inverse * (
+        scaled - normed * jnp.mean(scaled * normed, -1, keepdims=True)
+    )
+    grad_res[...] = result
+    branch = result.astype(jnp.bfloat16)
+    for line in range(lines):
+        out_term[:, line * cols : (line + 1) * cols] = matmul(
+            branch, attended_all[line, z], COLS_BY_COLS
+        ).astype(jnp.bfloat16)
+        attended_grad[line] = matmul(
+            branch, out_full[:, line * cols : (line + 1) * cols], ROWS_BY_COLS
+        ).astype(jnp.bfloat16)
+
+
+def exchange_kernel(blocks, swapped, local_sem, sends, recvs):
+    here = Place()
+    meet([here.line_peer(k) for k in range(1, here.lines)])
+    own = pltpu.make_async_copy(blocks.at[here.z], swapped.at[here.z], local_sem)
+    own.start()
+    swap = LineSwap(here, lambda z: blocks.at[z], lambda k: swapped.at[here.z], sends, recvs)
+    swap.start()
+    own.wait()
+    swap.finish()
+
+
+def attend_back_kernel(
+    prefix, tokens, att_in, weights, gain, cosine, sine_table, queries, keys, values, attended, log_total, attended_grad, qkv_term, in_part, joined_grad, key_sum, value_sum
+):
+    rows_all, width = tokens.shape
+    q_width, kv_width = queries.shape[1], keys.shape[1]
+    qkv_width = q_width + 2 * kv_width
+    heads = q_width // HEAD_WIDTH
+    group = q_width // kv_width
+    block = rows_all // lax.axis_size("seq")
+    prefix_end = prefix[0]
+    key_sum[...] = jnp.zeros_like(key_sum)
+    value_sum[...] = jnp.zeros_like(value_sum)
+    for start in range(0, rows_all, block):
+        here = pl.ds(start, block)
+        reach = max(rows_all // 2, start + block)
+        query_place = start + lax.broadcasted_iota(jnp.int32, (block, reach), 0)
+        key_place = lax.broadcasted_iota(jnp.int32, (block, reach), 1)
+        allowed = (key_place <= query_place) | (key_place < prefix_end)
+        query_grads = []
+        for head in range(heads):
+            own = slice(head * HEAD_WIDTH, (head + 1) * HEAD_WIDTH)
+            low = head // group * HEAD_WIDTH
+            shared = slice(low, low + HEAD_WIDTH)
+            query, key = queries[here, own], keys[:reach, shared]
+            grad = attended_grad[here, own]
+            scores = matmul(query, key, ROWS_BY_ROWS) * SCORE_SCALE
+            prob = jnp.where(allowed, jnp.exp(scores - log_total[here, head : head + 1]), 0.0)
+            delta = jnp.sum(grad.astype(jnp.float32) * attended[here, own], -1, keepdims=True)
+            prob_part = matmul(grad, values[:reach, shared], ROWS_BY_ROWS)
+            score_grad = (prob * (prob_part - delta)).astype(jnp.bfloat16)
+            value_sum[:reach, shared] = value_sum[:reach, shared] + matmul(
+                prob.astype(jnp.bfloat16), grad, COLS_BY_COLS
+            )
+            key_sum[:reach, shared] = key_sum[:reach, shared] + matmul(score_grad, query, COLS_BY_COLS)
+            query_grads.append(matmul(score_grad, key, ROWS_BY_COLS))
+        query_grad = jnp.concatenate(query_grads, 1) * SCORE_SCALE
+        joined_grad[here, :q_width] = spin(query_grad, cosine[here, :], -sine_table[here, :]).astype(
+            jnp.bfloat16
+        )
+    joined_grad[:, q_width : q_width + kv_width] = spin(
+        key_sum[...] * SCORE_SCALE, cosine[...], -sine_table[...]
+    ).astype(jnp.bfloat16)
+    joined_grad[:, q_width + kv_width :] = value_sum[...].astype(jnp.bfloat16)
+    qkv_term[:, :qkv_width] = matmul(att_in[...], joined_grad[...], COLS_BY_COLS).astype(jnp.bfloat16)
+    gain_term = jnp.zeros((width, LANES), jnp.float32)
+    for start in range(0, rows_all, block):
+        here = pl.ds(start, block)
+        hidden = tokens[here, :].astype(jnp.float32)
+        normed = hidden * lax.rsqrt(jnp.mean(hidden * hidden, -1, keepdims=True) + NORM_EPS)
+        part = matmul(joined_grad[here, :], weights[:, :qkv_width], ROWS_BY_ROWS)
+        in_part[here, :] = part.astype(jnp.bfloat16)
+        gain_term = gain_term + split_sum_columns(part * normed)
+    qkv_term[:, qkv_width:] = gain_term.astype(jnp.bfloat16)
+
+
+def tokens_kernel(in_part, grad_res, tokens, gain, tokens_grad, got, sends, recvs):
+    here = Place()
+    meet([here.line_peer(k) for k in range(1, here.lines)])
+    swap = LineSwap(here, lambda z: in_part.at[z], lambda k: got.at[k - 1], sends, recvs)
+    swap.start()
+    swap.finish()
+    total = in_part[here.z].astype(jnp.float32)
+    for k in range(here.lines - 1):
+        total = total + got[k].astype(jnp.float32)
+    hidden = tokens[...].astype(jnp.float32)
+    inverse = lax.rsqrt(jnp.mean(hidden * hidden, -1, keepdims=True) + NORM_EPS)
+    normed = hidden * inverse
+    scaled = total * gain[...]
+    tokens_grad[...] = grad_res[...] + inverse * (
+        scaled - normed * jnp.mean(scaled * normed, -1, keepdims=True)
+    )
+
+
+def reduce_kernel(
+    experts, outs, qkvs, expert_out, out_out, qkv_out,
+    e_core, e_sum, e_chips, e_half, e_line,
+    o_core, o_sum, o_chips, o_half, o_line,
+    q_core, q_sum, q_chips, q_half, q_line,
+    e_sends, e_recvs, o_sends, o_recvs, q_sends, q_recvs,
+):
+    here = Place()
+    meet(all_peers(here))
+    other = 1 - here.core
+    lines, chips = here.lines, here.chips
+    first = [
+        send(outs.at[:, other], o_core, o_sends.at[0], o_recvs.at[0], here.sibling()),
+        send(qkvs.at[:, other], q_core, q_sends.at[0], q_recvs.at[0], here.sibling()),
+        send(experts.at[:, :, other], e_core, e_sends.at[0], e_recvs.at[0], here.sibling()),
+    ]
+
+    def added(left, right):
+        return (left.astype(jnp.float32) + right.astype(jnp.float32)).astype(jnp.bfloat16)
+
+    def plane(total, received, sends, recvs, pick):
+        return [
+            send(
+                pick(total, (here.chip + k) % chips),
+                received.at[k - 1],
+                sends.at[k],
+                recvs.at[k],
+                here.chip_peer(k),
+            )
+            for k in range(1, chips)
+        ]
+
+    def line(half, received, sends, recvs, pick):
+        return [
+            send(
+                pick(half, (here.z + k) % lines),
+                received.at[k - 1],
+                sends.at[chips - 1 + k],
+                recvs.at[chips - 1 + k],
+                here.line_peer(k),
+            )
+            for k in range(1, lines)
+        ]
+
+    first[0].wait()
+    o_sum[...] = added(outs[:, here.core], o_core[...])
+    o_plane = plane(o_sum, o_chips, o_sends, o_recvs, lambda ref, chip: ref.at[chip])
+    first[1].wait()
+    q_sum[...] = added(qkvs[:, here.core], q_core[...])
+    q_plane = plane(q_sum, q_chips, q_sends, q_recvs, lambda ref, chip: ref.at[chip])
+    first[2].wait()
+    for expert in range(experts.shape[0]):
+        e_sum[expert] = added(experts[expert, :, here.core], e_core[expert])
+    e_plane = plane(e_sum, e_chips, e_sends, e_recvs, lambda ref, chip: ref.at[:, chip])
+
+    def collected(own, received):
+        total = own.astype(jnp.float32)
+        for k in range(chips - 1):
+            total = total + received(k).astype(jnp.float32)
+        return total.astype(jnp.bfloat16)
+
+    for copy in o_plane:
+        copy.wait()
+    o_half[...] = collected(o_sum[here.chip], lambda k: o_chips[k])
+    o_lines = line(o_half, o_line, o_sends, o_recvs, lambda ref, z: ref.at[z])
+    for copy in q_plane:
+        copy.wait()
+    q_half[...] = collected(q_sum[here.chip], lambda k: q_chips[k])
+    q_lines = line(q_half, q_line, q_sends, q_recvs, lambda ref, z: ref.at[z])
+    for copy in e_plane:
+        copy.wait()
+    for expert in range(experts.shape[0]):
+        e_half[expert] = collected(e_sum[expert, here.chip], lambda k: e_chips[k, expert])
+    e_lines = [
+        send(
+            e_half.at[:, (here.z + k) % lines],
+            e_line.at[here.z],
+            e_sends.at[chips - 1 + k],
+            e_recvs.at[chips - 1 + k],
+            here.line_peer(k),
+        )
+        for k in range(1, lines)
+    ]
+    for copy in o_lines:
+        copy.wait()
+    total = o_half[here.z].astype(jnp.float32)
+    for k in range(lines - 1):
+        total = total + o_line[k].astype(jnp.float32)
+    out_out[...] = total
+    for copy in q_lines:
+        copy.wait()
+    qkv_out[here.z] = q_half[here.z].astype(jnp.float32)
+    for k in range(1, lines):
+        qkv_out[(here.z + lines - k) % lines] = q_line[k - 1].astype(jnp.float32)
+    for copy in e_lines:
+        copy.wait()
+    e_line[here.z] = e_half[:, here.z]
+    expert_out[...] = e_line[...].astype(jnp.float32)
+
+
+def fast_device(
+    tokens, prefix_len, routes, cotangent, query_matrix, key_matrix, value_matrix, output_matrix,
+    attention_gain, expert_gain, router_matrix, gate_up_weight, down_weight,
+):
+    lines = lax.axis_size("seq")
+    chips = lax.axis_size("dp") // 2
+    tok_rows, width = tokens.shape[1:]
+    rows_all = lines * tok_rows
+    depth = query_matrix.shape[0]
+    query_width, key_width = query_matrix.shape[1], key_matrix.shape[1]
+    q_cols, kv_cols = query_width // lines, key_width // lines
+    qkv_cols = q_cols + 2 * kv_cols
+    expert_count = router_matrix.shape[1]
+    own_experts = expert_count // lines
+    ff_width = down_weight.shape[2]
+    all_ff = 3 * ff_width
+    row_cols = qkv_cols + LANES
+    half_dim = HEAD_WIDTH // 2
+
+    places = np.arange(rows_all, dtype=np.float32)
+    frequency = np.exp(
+        np.arange(half_dim, dtype=np.float32) * np.float32(-2.0 * math.log(10000.0) / HEAD_WIDTH)
+    ).astype(np.float32)
+    angles = places[:, None] * frequency[None, :]
+    cosine = jnp.asarray(np.tile(np.cos(angles), (1, LANES // half_dim)), jnp.float32)
+    sine_table = jnp.asarray(np.tile(np.sin(angles), (1, LANES // half_dim)), jnp.float32)
+
+    def by_line(matrix, cols):
+        return matrix.reshape(depth, lines, cols).transpose(1, 0, 2)
+
+    small = jnp.concatenate(
+        [router_matrix, attention_gain[:, None], expert_gain[:, None],
+         jnp.zeros((depth, LANES - expert_count - 2), jnp.bfloat16)], 1,
+    )
+    rows = jnp.concatenate(
+        [by_line(query_matrix, q_cols), by_line(key_matrix, kv_cols), by_line(value_matrix, kv_cols),
+         jnp.broadcast_to(small[None], (lines, depth, LANES))], 2,
+    )
+    DMA = pltpu.SemaphoreType.DMA
+    count = spread_count(lines, chips)
+    tokens_all, weights = pl.pallas_call(
+        front_kernel,
+        name="front",
+        out_shape=(shape_of(lines, tok_rows, width), shape_of(chips, 2, lines, depth, row_cols)),
+        in_specs=[ANY_SPEC] * 2,
+        out_specs=(ANY_SPEC,) * 2,
+        scratch_shapes=[DMA((2,)), DMA((count,)), DMA((count,)), DMA((lines,)), DMA((lines,))],
+        compiler_params=comm_params(1),
+    )(tokens[0], rows)
+    weights = weights.reshape(width, row_cols)
+    gains = weights[:, qkv_cols + expert_count : qkv_cols + expert_count + 2].astype(jnp.float32).T
+    gain_attention, gain_expert = gains[0:1], gains[1:2]
+    router = weights[:, qkv_cols:]
+    router = jnp.where(jnp.arange(LANES)[None, :] < expert_count, router, 0)
+    tokens_all = tokens_all.reshape(rows_all, width)
+
+    att_in, queries, keys, values, attended, attended_low, log_total = pl.pallas_call(
+        attend_kernel,
+        name="attend",
+        out_shape=(
+            shape_of(rows_all, width), shape_of(rows_all, q_cols), shape_of(rows_all, kv_cols), shape_of(rows_all, kv_cols),
+            shape_of(rows_all, q_cols, kind=jnp.float32), shape_of(rows_all, q_cols), shape_of(rows_all, LANES, kind=jnp.float32),
+        ),
+        in_specs=[SMEM_SPEC] + [VMEM_SPEC] * 5,
+        out_specs=(VMEM_SPEC,) * 7,
+        compiler_params=pltpu.CompilerParams(vmem_limit_bytes=56 << 20),
+    )(prefix_len, tokens_all, weights, gain_attention, cosine, sine_table)
+
+    attended_all = pl.pallas_call(
+        gather_kernel,
+        name="attended_gather",
+        out_shape=shape_of(lines, rows_all, q_cols),
+        in_specs=[ANY_SPEC],
+        out_specs=ANY_SPEC,
+        scratch_shapes=[DMA(()), DMA((lines,)), DMA((lines,))],
+        compiler_params=comm_params(2),
+    )(attended_low)
+
+    chosen = jnp.sum(
+        (routes[0][:, :, None] == jnp.arange(LANES, dtype=jnp.int32)[None, None, :]).astype(jnp.bfloat16), 1
+    )
+    marked = jnp.concatenate([cotangent[0], chosen], 1)
+    expert_rows = jnp.concatenate([gate_up_weight, down_weight], 2).transpose(1, 0, 2)
+    expert_rows = expert_rows.reshape(lines, own_experts, depth, all_ff)
+    out_full, expert_full, marked_all = pl.pallas_call(
+        supply_kernel,
+        name="supply",
+        out_shape=(
+            shape_of(chips, 2, lines, depth, query_width),
+            shape_of(own_experts, chips, 2, lines, depth, all_ff),
+            shape_of(lines, tok_rows, width + LANES),
+        ),
+        in_specs=[ANY_SPEC] * 3,
+        out_specs=(ANY_SPEC,) * 3,
+        scratch_shapes=[DMA((3,))] + [DMA((count,))] * 4 + [DMA((lines,))] * 2,
+        compiler_params=comm_params(3),
+    )(output_matrix, expert_rows, marked)
+    out_full = out_full.reshape(width, query_width)
+    expert_full = expert_full.reshape(own_experts, width, all_ff)
+    marked_all = marked_all.reshape(rows_all, width + LANES)
+
+    expert_in, probs, middle = pl.pallas_call(
+        middle_kernel,
+        name="middle",
+        out_shape=(
+            shape_of(rows_all, width), shape_of(rows_all, LANES, kind=jnp.float32), shape_of(rows_all, width, kind=jnp.float32),
+        ),
+        in_specs=[VMEM_SPEC] * 5,
+        out_specs=(VMEM_SPEC,) * 3,
+        compiler_params=pltpu.CompilerParams(vmem_limit_bytes=56 << 20),
+    )(tokens_all, attended_all, out_full, gain_expert, router)
+
+    whole = lambda *dims: pl.BlockSpec(dims, lambda e: (0,) * len(dims))
+    each = pl.BlockSpec((1, width, all_ff), lambda e: (e, 0, 0))
+    mixed_part, in_grad, gate_grad, expert_grad = pl.pallas_call(
+        expert_kernel,
+        name="experts",
+        grid=(own_experts,),
+        out_shape=(
+            shape_of(rows_all, width), shape_of(rows_all, width), shape_of(rows_all, LANES, kind=jnp.float32),
+            shape_of(own_experts, width, all_ff),
+        ),
+        in_specs=[whole(rows_all, width), whole(rows_all, width + LANES), whole(rows_all, LANES), each],
+        out_specs=(whole(rows_all, width), whole(rows_all, width), whole(rows_all, LANES), each),
+        scratch_shapes=[pltpu.VMEM((rows_all, width), jnp.float32)] * 2,
+        compiler_params=pltpu.CompilerParams(vmem_limit_bytes=56 << 20, dimension_semantics=("arbitrary",)),
+    )(expert_in, marked_all, probs, expert_full)
+
+    line_shape = (lines, tok_rows)
+    mixed, in_total, gate_total = pl.pallas_call(
+        settle_kernel,
+        name="settle",
+        out_shape=(
+            shape_of(tok_rows, width), shape_of(tok_rows, width, kind=jnp.float32), shape_of(tok_rows, LANES, kind=jnp.float32),
+        ),
+        in_specs=[VMEM_SPEC] * 4,
+        out_specs=(VMEM_SPEC,) * 3,
+        scratch_shapes=[
+            pltpu.VMEM((lines - 1, tok_rows, width), jnp.bfloat16), pltpu.VMEM((lines - 1, tok_rows, width), jnp.bfloat16),
+            pltpu.VMEM((lines - 1, tok_rows, LANES), jnp.float32),
+        ] + [DMA((lines,))] * 6,
+        compiler_params=comm_params(4),
+    )(mixed_part.reshape(*line_shape, width), in_grad.reshape(*line_shape, width), gate_grad.reshape(*line_shape, LANES),
+      middle.reshape(*line_shape, width))
+
+    grad_res, out_term, attended_grad = pl.pallas_call(
+        branch_kernel,
+        name="branch",
+        out_shape=(
+            shape_of(tok_rows, width, kind=jnp.float32), shape_of(width, query_width + LANES), shape_of(lines, tok_rows, q_cols),
+        ),
+        in_specs=[VMEM_SPEC] * 10,
+        out_specs=(VMEM_SPEC,) * 3,
+        compiler_params=pltpu.CompilerParams(vmem_limit_bytes=56 << 20),
+    )(in_total, gate_total, probs.reshape(*line_shape, LANES), expert_in.reshape(*line_shape, width), cotangent[0],
+      middle.reshape(*line_shape, width), gain_expert, router, attended_all.reshape(lines, lines, tok_rows, q_cols), out_full)
+
+    attended_grad = pl.pallas_call(
+        exchange_kernel,
+        name="exchange",
+        out_shape=shape_of(lines, tok_rows, q_cols),
+        in_specs=[ANY_SPEC],
+        out_specs=ANY_SPEC,
+        scratch_shapes=[DMA(()), DMA((lines,)), DMA((lines,))],
+        compiler_params=comm_params(5),
+    )(attended_grad).reshape(rows_all, q_cols)
+
+    qkv_term, in_part = pl.pallas_call(
+        attend_back_kernel,
+        name="attend_back",
+        out_shape=(shape_of(width, row_cols), shape_of(rows_all, width)),
+        in_specs=[SMEM_SPEC] + [VMEM_SPEC] * 12,
+        out_specs=(VMEM_SPEC,) * 2,
+        scratch_shapes=[
+            pltpu.VMEM((rows_all, qkv_cols), jnp.bfloat16), pltpu.VMEM((rows_all, kv_cols), jnp.float32),
+            pltpu.VMEM((rows_all, kv_cols), jnp.float32),
+        ],
+        compiler_params=pltpu.CompilerParams(vmem_limit_bytes=56 << 20),
+    )(prefix_len, tokens_all, att_in, weights, gain_attention, cosine, sine_table, queries, keys, values, attended, log_total, attended_grad)
+
+    tokens_grad = pl.pallas_call(
+        tokens_kernel,
+        name="tokens_grad",
+        out_shape=shape_of(tok_rows, width, kind=jnp.float32),
+        in_specs=[VMEM_SPEC] * 4,
+        out_specs=VMEM_SPEC,
+        scratch_shapes=[pltpu.VMEM((lines - 1, tok_rows, width), jnp.bfloat16)] + [DMA((lines,))] * 2,
+        compiler_params=comm_params(6),
+    )(in_part.reshape(*line_shape, width), grad_res, tokens[0], gain_attention)
+
+    def buffers(cols, lead=()):
+        low = jnp.bfloat16
+        return [
+            pltpu.VMEM((*lead, chips, lines, depth, cols), low), pltpu.VMEM((*lead, chips, lines, depth, cols), low),
+            pltpu.VMEM((chips - 1, *lead, lines, depth, cols), low), pltpu.VMEM((*lead, lines, depth, cols), low),
+        ]
+
+    steps = chips + lines
+    expert_sum, out_sum, qkv_sum = pl.pallas_call(
+        reduce_kernel,
+        name="reduce",
+        out_shape=(
+            shape_of(lines, own_experts, depth, all_ff, kind=jnp.float32), shape_of(depth, query_width + LANES, kind=jnp.float32),
+            shape_of(lines, depth, row_cols, kind=jnp.float32),
+        ),
+        in_specs=[VMEM_SPEC] * 3,
+        out_specs=(VMEM_SPEC,) * 3,
+        scratch_shapes=buffers(all_ff, (own_experts,)) + [pltpu.VMEM((lines, own_experts, depth, all_ff), jnp.bfloat16)]
+        + buffers(query_width + LANES) + [pltpu.VMEM((lines - 1, depth, query_width + LANES), jnp.bfloat16)]
+        + buffers(row_cols) + [pltpu.VMEM((lines - 1, depth, row_cols), jnp.bfloat16)]
+        + [DMA((steps,))] * 6,
+        compiler_params=comm_params(7, 60),
+    )(expert_grad.reshape(own_experts, chips, 2, lines, depth, all_ff), out_term.reshape(chips, 2, lines, depth, query_width + LANES),
+      qkv_term.reshape(chips, 2, lines, depth, row_cols))
+
+    def joined(start, cols):
+        return qkv_sum[:, :, start : start + cols].transpose(1, 0, 2).reshape(depth, lines * cols)
+
+    expert_sum = expert_sum.reshape(expert_count, depth, all_ff)
+    return (
+        mixed[None],
+        tokens_grad[None],
+        joined(0, q_cols),
+        joined(q_cols, kv_cols),
+        joined(q_cols + kv_cols, kv_cols),
+        out_sum[:, :query_width],
+        jnp.sum(qkv_sum[:, :, qkv_cols], 0),
+        out_sum[:, query_width + expert_count],
+        out_sum[:, query_width : query_width + expert_count],
+        expert_sum[:, :, : 2 * ff_width].transpose(1, 0, 2),
+        expert_sum[:, :, 2 * ff_width :].transpose(1, 0, 2),
+    )
+
+
 def solution(mesh):
+    lines, chips = mesh.shape["seq"], mesh.shape["dp"] // 2
+    even = KEY_HEADS % (2 * lines) == 0 and EXPERT_COUNT % lines == 0 and mesh.shape["dp"] == 2 * chips
     return jax.shard_map(
-        per_device,
+        fast_device if even else per_device,
         mesh=mesh,
         in_specs=(
             P("dp", "seq", None),

time: 2300 us -> 514 us (0.22)
  waiting for transfers between devices: 1620 us -> 0 us
  Pallas kernels: 0 us -> 475 us
  blocking collectives: 179 us -> 0 us
  other arithmetic: 161 us -> 8.24 us
  local copies, waits for them, and re-layouts: 167 us -> 22.8 us
  matrix products: 143 us -> 0 us
    reduce_scatter x5 -> x0, waiting for transfers between devices: 1310 us -> none  [the longest x1 738 us: per_device(): lax.psum_scatter(jnp.concatenate([gate_up_term, down_term], axis=-1), ('d...]
    pallas_call x0 -> x12, Pallas kernels: none -> 475 us  [the longest x1 134 us: fast_device(): pl.pallas_call(reduce_kernel, name='reduce', out_shape=(shape_of(lines, o...]
    all_gather x6 -> x0, waiting for transfers between devices: 307 us -> none  [the longest x1 188 us: per_device(): lax.all_gather(gate_up_weight, ('dp', 'seq'), axis=0, tiled=True)]
    dot_general x27 -> x0, matrix products: 142 us -> none  [the longest x1 25.9 us: per_device(): jnp.einsum('ecd,ecf->def', dispatched, mid_grad, preferred_element_type=j...]
    concatenate x2 -> x1, local copies, waits for them, and re-layouts: 100 us -> 0.08 us  [fast_device(): jnp.concatenate([router_matrix, attention_gain[:, None], expert_gain[:, N...]
    all_gather x3 -> x0, blocking collectives: 98.6 us -> none  [the longest x1 67.3 us: per_device(): lax.all_gather(router_matrix, ('dp', 'seq'), axis=0, tiled=True)]
    unnamed x2 -> x0, blocking collectives: 80.8 us -> none
    concatenate x4 -> x3, other arithmetic: 67.5 us -> 2.46 us  [the longest x1 1.69 us: fast_device(): marked = jnp.concatenate([cotangent[0], chosen], 1)]
  transfers between devices with their start and end apart: 14 -> 0, of which waited for: 8 -> 0; matrix products, arithmetic and copies ran while one was open for 16% -> 0% of each run, Pallas kernels for 0% -> 0%
where the time goes in v1:
time: 514 us; the launch traced here: 507 us
  Pallas kernels  475 us (92%)
  local copies, waits for them, and re-layouts  22.8 us (4%)
  other arithmetic  8.24 us (2%)
    pallas_call x1, Pallas kernels, fast_device(): pl.pallas_call(reduce_kernel, name='reduce', out_shape=(shape_of(lines, o...  134 us
    pallas_call x1, Pallas kernels, fast_device(): pl.pallas_call(supply_kernel, name='supply', out_shape=(shape_of(chips, 2...  113 us
    pallas_call x1, Pallas kernels, fast_device(): pl.pallas_call(settle_kernel, name='settle', out_shape=(shape_of(tok_rows...  73.8 us
    pallas_call x1, Pallas kernels, fast_device(): pl.pallas_call(front_kernel, name='front', out_shape=(shape_of(lines, tok...  29 us
    pallas_call x1, Pallas kernels, fast_device(): pl.pallas_call(expert_kernel, name='experts', grid=(own_experts,), out_sh...  28.1 us
    pallas_call x1, Pallas kernels, fast_device(): pl.pallas_call(gather_kernel, name='attended_gather', out_shape=shape_of(...  24.4 us
    pallas_call x1, Pallas kernels, fast_device(): pl.pallas_call(tokens_kernel, name='tokens_grad', out_shape=shape_of(tok_...  23.9 us
    pallas_call x1, Pallas kernels, fast_device(): pl.pallas_call(exchange_kernel, name='exchange', out_shape=shape_of(lines...  13.9 us

profile of v1, /device:TPU:0, one launch (start us, length us, event | category | flops | bytes accessed | tf_op | source)
XLA Modules:
  0.0 507.1 jit_solution(616269551399390581)
XLA Ops:
  7.2 1.7 pad_maximum_fusion.marked
  8.9 1.2 maximum_bitcast_fusion
  10.1 2.0 copy.61
  12.1 29.0 %front.1 = (bf16[4,128,1024]{2,1,0:T(8,128)(2,1)}, bf16[4,2,4,32,640]{4,3,2,1,0:T(8,128)(2,1)}) custom-call(bf16[128,1024]{1,0:T(8,128)(2,1)} %bitcast.101, bf16[4,32,640]{2,1,0:T(8,128)(2,1)} %pad_maximum_fusion.1.rows), custom_call_target="tpu_custom_call" | custom-call | tf_op jit(solution)/shard_map/front/pallas_call | solution.py:1094
  41.1 1.7 slice_select_fusion.router
  42.8 1.1 slice_convert_fusion
  44.6 6.8 %attend.1 = (bf16[512,1024]{1,0:T(8,128)(2,1)}, bf16[512,256]{1,0:T(8,128)(2,1)}, bf16[512,128]{1,0:T(8,128)(2,1)}, bf16[512,128]{1,0:T(8,128)(2,1)}, f32[512,25...) custom-call(s32[1]{0:T(128)S(6)} %copy.93.prefix, bf16[512,1024]{1,0:T(8,128)(2,1)} %bitcast.75, ...), custom_call_target="tpu_custom_call" | custom-call | tf_op jit(solution)/shard_map/attend/pallas_call | solution.py:1110
  51.4 24.4 %attended_gather.1.attended_all = bf16[4,512,256]{2,1,0:T(8,128)(2,1)} custom-call(bf16[512,256]{1,0:T(8,128)(2,1)} %get-tuple-element.43.block), custom_call_target="tpu_custom_call" | custom-call | tf_op jit(solution)/shard_map/attended_gather/pallas_call | solution.py:1122
  75.8 113.3 %supply.1 = (bf16[4,2,4,32,1024]{4,3,2,1,0:T(8,128)(2,1)}, bf16[4,4,2,4,32,1536]{5,4,3,2,1,0:T(8,128)(2,1)}, bf16[4,128,1152]{2,1,0:T(8,128)(2,1)}) custom-call(bf16[32,1024]{1,0:T(8,128)(2,1)} %out_rows.1, bf16[4,4,32,1536]{3,2,1,0:T(8,128)(2,1)} %bitcast.86, bf16[128,1152]{1,0:T(8,128)(2,1)} %pad_maximum_fusion.marked), custom_call_target="tpu_custom_call" | custom-call | tf_op jit(solution)/shard_map/supply/pallas_call | solution.py:1138
  189.1 7.8 %middle.1 = (bf16[512,1024]{1,0:T(8,128)(2,1)}, f32[512,128]{1,0:T(8,128)}, f32[512,1024]{1,0:T(8,128)}) custom-call(bf16[512,1024]{1,0:T(8,128)(2,1)} %bitcast.76, bf16[4,512,256]{2,1,0:T(8,128)(2,1)} %attended_gather.1.attended_all, bf16[1024,1024]{1,0:T(8,128)(2,1)} %bitcast.78, f32[1,1024]{1,0:T(1,128)} %get-tuple-element.106.gain, ...), custom_call_target="tpu_custom_call" | custom-call | tf_op jit(solution)/shard_map/middle/pallas_call | solution.py:1155
  197.0 28.1 %experts.1 = (bf16[512,1024]{1,0:T(8,128)(2,1)}, bf16[512,1024]{1,0:T(8,128)(2,1)}, f32[512,128]{1,0:T(8,128)}, bf16[4,1024,1536]{2,1,0:T(8,128)(2,1)}) custom-call(bf16[512,1024]{1,0:T(8,128)(2,1)} %get-tuple-element.45.expert_in, bf16[512,1152]{1,0:T(8,128)(2,1)} %bitcast.94, f32[512,128]{1,0:T(8,128)} %get-tuple-element.47.probs, ...), custom_call_target="tpu_custom_call" | custom-call | tf_op jit(solution)/shard_map/experts/pallas_call | solution.py:1168
  225.1 73.8 %settle.1 = (bf16[128,1024]{1,0:T(8,128)(2,1)}, f32[128,1024]{1,0:T(8,128)}, f32[128,128]{1,0:T(8,128)}) custom-call(bf16[4,128,1024]{2,1,0:T(8,128)(2,1)} %bitcast.96, bf16[4,128,1024]{2,1,0:T(8,128)(2,1)} %bitcast.97, f32[4,128,128]{2,1,0:T(8,128)} %bitcast.105, f32[4,128,1024]{2,1,0:T(8,128)} %bitcast.80), custom_call_target="tpu_custom_call" | custom-call | tf_op jit(solution)/shard_map/settle/pallas_call | solution.py:1183
  298.9 6.4 %branch.1 = (f32[128,1024]{1,0:T(8,128)}, bf16[1024,1152]{1,0:T(8,128)(2,1)}, bf16[4,128,256]{2,1,0:T(8,128)(2,1)}) custom-call(f32[128,1024]{1,0:T(8,128)} %get-tuple-element.60.in_total, f32[128,128]{1,0:T(8,128)} %get-tuple-element.61.gate_total, f32[4,128,128]{2,1,0:T(8,128)} %bitcast.95, bf16[4,128,1024]{2,1,0:T(8,128)(2,1)} %bitcast.87, ...), custom_call_target="tpu_custom_call" | custom-call | tf_op jit(solution)/shard_map/branch/pallas_call | solution.py:1199
  305.3 13.9 %exchange.1 = bf16[4,128,256]{2,1,0:T(8,128)(2,1)} custom-call(bf16[4,128,256]{2,1,0:T(8,128)(2,1)} %get-tuple-element.62.blocks), custom_call_target="tpu_custom_call" | custom-call | tf_op jit(solution)/shard_map/exchange/pallas_call | solution.py:1211
  319.2 13.4 %attend_back.1 = (bf16[1024,640]{1,0:T(8,128)(2,1)}, bf16[512,1024]{1,0:T(8,128)(2,1)}) custom-call(s32[1]{0:T(128)S(6)} %copy.93.prefix, bf16[512,1024]{1,0:T(8,128)(2,1)} %bitcast.77, bf16[512,1024]{1,0:T(8,128)(2,1)} %get-tuple-element.54.att_in, bf16[1024,640]{1,0:T(8,128)(2,1)} %bitcast.85, f32[1,1024]{1,0:T(1,128)} %get-tuple-element.107.gain, ...), custom_call_target="tpu_custom_call" | custom-call | tf_op jit(solution)/shard_map/attend_back/pallas_call | solution.py:1221
  332.6 23.9 %tokens_grad.1 = f32[128,1024]{1,0:T(8,128)} custom-call(bf16[4,128,1024]{2,1,0:T(8,128)(2,1)} %bitcast.104, f32[128,1024]{1,0:T(8,128)} %get-tuple-element.64.grad_res, bf16[128,1024]{1,0:T(8,128)(2,1)} %bitcast.102, f32[1,1024]{1,0:T(1,128)} %get-tuple-element.107.gain), custom_call_target="tpu_custom_call" | custom-call | tf_op jit(solution)/shard_map/tokens_grad/pallas_call | solution.py:1234
  356.5 133.8 %reduce.5 = (f32[4,4,32,1536]{3,2,1,0:T(8,128)}, f32[32,1152]{1,0:T(8,128)}, f32[4,32,640]{2,1,0:T(8,128)}) custom-call(bf16[4,4,2,4,32,1536]{5,4,3,2,1,0:T(8,128)(2,1)} %bitcast.73, bf16[4,2,4,32,1152]{4,3,2,1,0:T(8,128)(2,1)} %bitcast.90, bf16[4,2,4,32,640]{4,3,2,1,0:T(8,128)(2,1)} %bitcast.93), custom_call_target="tpu_custom_call" | custom-call | tf_op jit(solution)/shard_map/reduce/pallas_call | solution.py:1252
  490.3 1.6 slice_reduce_fusion
  491.9 1.4 slice_reduce_fusion.1
  494.0 1.6 slice.46
  496.3 0.9 slice_bitcast_fusion
  500.0 1.3 slice.57
  501.5 2.5 copy.86
  504.1 1.6 copy.87
  (34 shorter events, 12.5 us)
Async XLA Ops:
  0.6 5.1 %copy-start = (bf16[32,512]{1,0:T(8,128)(2,1)S(1)}, bf16[32,512]{1,0:T(8,128)(2,1)}, u32[]{:S(2)}) copy-start(bf16[32,512]{1,0:T(8,128)(2,1)} %param.20) | copy-start | bytes 98308
  0.7 8.2 %copy-start.3 = (bf16[32,16,1024]{2,1,0:T(8,128)(2,1)S(1)}, bf16[32,16,1024]{2,1,0:T(8,128)(2,1)}, u32[]{:S(2)}) copy-start(bf16[32,16,1024]{2,1,0:T(8,128)(2,1)} %param.26) | copy-start | bytes 3145732
  490.3 11.1 %copy-start.1 = (f32[4,4,32,1536]{3,2,1,0:T(8,128)S(1)}, f32[4,4,32,1536]{3,2,1,0:T(8,128)}, u32[]{:S(2)}) copy-start(f32[4,4,32,1536]{3,2,1,0:T(8,128)} %get-tuple-element.70) | copy-start | bytes 9437188
  504.1 1.6 copy-start.4
  504.1 2.3 copy-start.2
